TPU v7x, 32 devices: a whole 2x2x4 slice. The times are simulated.
32 devices in a mesh: groups: 2 (over y), qry: 4 (over x, core), ref: 4 (over z).
Axes of the slice: x: 2, y: 2, z: 4, core: 2. Of those that a mesh axis runs over, the one named last changes fastest.
Arguments:
- query_feats: bfloat16 [1024, 9, 3840], P(('groups', 'qry')), parts along dimension 0, may hold values from -6 to 6
- ref_feats: bfloat16 [256, 4, 9, 3840], P(('groups', 'ref'), 'qry'), parts along dimension 0, may hold values from -6 to 6
- pair_table: int32 [8, 4], P('groups'), parts along dimension 0, may hold values from 0 to 1, as said below
- lengths: int32 [4], P('groups'), parts along dimension 0, may hold values from 1 to 96, 128 in all
- query_len: int32 [2], P('groups'), parts along dimension 0, may hold values from 64 to 128
- conv1_weight: float32 [3, 3, 32], replicated, may hold values from -2 to 2
- conv1_bias: float32 [32], replicated, may hold values from -3 to 3
- conv2_weight: bfloat16 [3, 3, 64, 32], replicated, may hold values from -0.375 to 0.375
- conv2_bias: float32 [64], replicated, may hold values from -3 to 3
- conv3_weight: bfloat16 [3, 3, 128, 64], replicated, may hold values from -0.25 to 0.25
- conv3_bias: float32 [128], replicated, may hold values from -3 to 3
- conv4_weight: bfloat16 [128], replicated, may hold values from -0.5 to 0.5
- conv4_bias: float32 [1], replicated, may hold values from -3 to 3
Outputs:
- score_map: float32 [256, 128], P(('groups', 'qry'), 'ref'), parts along dimension 0
- video_scores: float32 [4], P('groups'), parts along dimension 0
There are 2 independent parts, one for each index of `groups`. A program takes and returns all parts, laid end to end along the dimension named above; an argument that names none is the same for every part. Nothing has to cross between parts.
Inputs may be any that keep to these rules, and one draw needn't show every extreme that they name: `pair_table`: in each row, at most 1 of the 1 tiles in the block of one index of ref are 1, and some such block holds exactly 1 in every draw.
All inputs are finite; a program needn't handle non-finite values.
Results may differ from a plain program's by a relative error of at most 0.01.
Values may be sent and summed in bfloat16 or wider, within the bound.
No kernel may reach another device: no remote copies, remote signals or barrier semaphores. Data moves between devices by JAX's collectives and lax.ppermute only.
A program may use at most 128 MiB of HBM per device.

v0:
```python
import math
import jax
import jax.numpy as jnp
from jax import lax
from jax.sharding import PartitionSpec as P

MOST = 1


def padded_2(block, sides, width):
    for axis, dim in sides:
        count = lax.axis_size(axis)
        forward = [(i, i + 1) for i in range(count - 1)]
        backward = [(target, source) for source, target in forward]
        low = lax.ppermute(
            lax.slice_in_dim(block, block.shape[dim] - width, None, axis=dim), axis, forward
        )
        high = lax.ppermute(lax.slice_in_dim(block, 0, width, axis=dim), axis, backward)
        block = jnp.concatenate([low, block, high], axis=dim)
    return block


def slot_table(mask, most):
    width = mask.shape[-1]
    ranking = jnp.cumsum(mask, axis=-1) - 1
    slot_ids = jnp.arange(most, dtype=jnp.int32)
    chosen = (mask[..., None, :] == 1) & (ranking[..., None, :] == slot_ids[:, None])
    picked = jnp.sum(jnp.where(chosen, jnp.arange(width, dtype=jnp.int32), 0), axis=-1)
    return (chosen, picked)


def frame_sims(query_mat, ref_mat, regions):
    products = lax.dot_general(
        query_mat, ref_mat, (((1,), (1,)), ((), ())), preferred_element_type=jnp.float32
    )
    frames = query_mat.shape[0] // regions
    others = ref_mat.shape[0] // regions
    best = jnp.max(products.reshape(frames, regions, others, regions), axis=3)
    return jnp.sum(best, axis=1) * (1.0 / (regions * math.sqrt(query_mat.shape[1])))


def conv_layer(padded, weights, bias, block_rows, use_pool):
    channels = padded.shape[0]
    height = padded.shape[1] - 2
    width = padded.shape[2] - 2
    block_rows = math.gcd(height, block_rows)
    outputs = weights.shape[0]
    accuracy = lax.Precision.HIGHEST if padded.dtype == jnp.float32 else None

    def one_block(position):
        window = lax.dynamic_slice_in_dim(padded, position * block_rows, block_rows + 2, 1)
        stacked = jnp.concatenate(
            [
                window[:, shift_row : shift_row + block_rows, shift_col : shift_col + width]
                for shift_row in range(3)
                for shift_col in range(3)
            ],
            axis=0,
        )
        result = jnp.dot(
            weights,
            stacked.reshape(9 * channels, block_rows * width),
            preferred_element_type=jnp.float32,
            precision=accuracy,
        )
        result = (result + bias[:, None]).reshape(outputs, block_rows, width)
        result = jnp.maximum(result, 0.0)
        if use_pool:
            result = jnp.max(
                result.reshape(outputs, block_rows // 2, 2, width // 2, 2), axis=(2, 4)
            )
        return result

    blocks = lax.map(one_block, jnp.arange(height // block_rows, dtype=jnp.int32))
    return jnp.transpose(blocks, (1, 0, 2, 3)).reshape(outputs, -1, blocks.shape[-1])


def weight_matrix(weight):
    return jnp.transpose(weight, (2, 0, 1, 3)).reshape(weight.shape[2], -1)


def body(
    query_feats,
    ref_feats,
    pair_table,
    lengths,
    query_len,
    conv1_weight,
    conv1_bias,
    conv2_weight,
    conv2_bias,
    conv3_weight,
    conv3_bias,
    conv4_weight,
    conv4_bias,
):
    qry_index = lax.axis_index("qry")
    ref_index = lax.axis_index("ref")
    frames = query_feats.shape[0]
    regions = query_feats.shape[1]
    channels = query_feats.shape[2]
    tiles_here = pair_table.shape[1] // lax.axis_size("ref")
    tile_rows = ref_feats.shape[0] // tiles_here
    query_mat = query_feats.reshape(frames * regions, channels)
    own_mask = lax.dynamic_slice(pair_table, (qry_index, ref_index * tiles_here), (1, tiles_here))[
        0
    ]
    chosen, picked = slot_table(own_mask, MOST)
    shards = lax.all_gather(ref_feats, "qry", axis=1, tiled=True)
    senders = shards.shape[1]
    sims = frame_sims(query_mat, shards.reshape(tile_rows * senders * regions, channels), regions)
    sims = sims.reshape(1, frames, tile_rows, senders)
    tile_sims = sims.reshape(MOST, frames, frames)
    placed = jnp.einsum(
        "st,sqf->qtf", chosen.astype(jnp.float32), tile_sims, precision=lax.Precision.HIGHEST
    )
    sim_map = placed.reshape(frames, tiles_here * frames)
    padded = padded_2(sim_map, (("qry", 0), ("ref", 1)), 1)
    first_weights = jnp.transpose(conv1_weight, (2, 0, 1)).reshape(conv1_weight.shape[2], 9)
    first = conv_layer(padded[None], first_weights, conv1_bias, 32, True).astype(jnp.bfloat16)
    padded = padded_2(first, (("qry", 1), ("ref", 2)), 1)
    second = conv_layer(padded, weight_matrix(conv2_weight), conv2_bias, 16, True).astype(
        jnp.bfloat16
    )
    padded = padded_2(second, (("qry", 1), ("ref", 2)), 1)
    third = conv_layer(padded, weight_matrix(conv3_weight), conv3_bias, 16, False).astype(
        jnp.bfloat16
    )
    map_rows = third.shape[1]
    map_cols = third.shape[2]
    score_map = (
        jnp.dot(
            conv4_weight[None],
            third.reshape(third.shape[0], -1),
            preferred_element_type=jnp.float32,
        ).reshape(map_rows, map_cols)
        + conv4_bias[0]
    )
    ends = jnp.cumsum(lengths)
    starts = ends - lengths
    column = ref_index * map_cols + jnp.arange(map_cols, dtype=jnp.int32)
    member = (column[:, None] >= starts[None, :]) & (column[:, None] < ends[None, :])
    peaks = jnp.max(jnp.where(member[None], score_map[:, :, None], -jnp.inf), axis=1)
    peaks = lax.pmax(peaks, "ref")
    row_ids = qry_index * map_rows + jnp.arange(map_rows, dtype=jnp.int32)
    partial_value = jnp.sum(jnp.where((row_ids < query_len[0])[:, None], peaks, 0.0), axis=0)
    totals = lax.psum(partial_value, "qry")
    return (score_map, totals / query_len[0].astype(jnp.float32))


def solution(mesh):
    placed = (
        P(("groups", "qry"), None, None),
        P(("groups", "ref"), "qry", None, None),
        P("groups", None),
        P("groups"),
        P("groups"),
        P(),
        P(),
        P(),
        P(),
        P(),
        P(),
        P(),
        P(),
    )
    return jax.shard_map(
        body,
        mesh=mesh,
        in_specs=placed,
        out_specs=(P(("groups", "qry"), "ref"), P("groups")),
        check_vma=False,
    )
```

profile of v0, /device:TPU:0, one launch (start us, length us, event | category | flops | bytes accessed | tf_op | source)
XLA Modules:
  0.0 248.4 jit_solution(3101193552977106752)
XLA Ops:
  7.2 0.7 all-gather.2.cloned.1.call-update
  7.9 1.3 dynamic_slice.23
  10.5 62.7 %all-gather.2.cloned.1.call-done = bf16[32,4,9,3840]{3,0,2,1:T(8,128)(2,1)} async-done(((bf16[32,1,9,3840]{3,0,2,1:T(8,128)(2,1)}), bf16[32,4,9,3840]{3,0,2,1:T(8,128)(2,1)}) %all-gather.2.cloned.1.call-update) | async-done | bytes 8847376 | tf_op jit(solution)/shard_map/all_gather | solution.py:109
  73.2 8.6 %copy.62 = bf16[32,4,9,3840]{3,1,0,2:T(4,128)(2,1)} copy(bf16[32,4,9,3840]{3,0,2,1:T(8,128)(2,1)} %all-gather.2.cloned.1.call-done) | data formatting | bytes 17694720 | tf_op jit(solution)/shard_map/all_gather | solution.py:109
  81.8 12.7 %reshape.195 = bf16[128,9,3840,1]{2,0,1,3:T(8,128)(2,1)} reshape(bf16[32,4,9,3840]{3,1,0,2:T(4,128)(2,1)} %copy.62) | data formatting | bytes 17694720 | tf_op jit(solution)/shard_map/dot_general | solution.py:33
  94.5 18.8 %fusion.7 = f32[128,9,128]{2,0,1:T(8,128)S(1)} fusion(bf16[128,9,3840,1]{2,0,1,3:T(8,128)(2,1)} %reshape.195, bf16[128,9,3840]{2,0,1:T(8,128)(2,1)} %param.19), kind=kOutput, calls=%fused_computation.40 | convolution fusion | flops 10193338368 | bytes 18284544 | tf_op jit(solution)/shard_map/dot_general | solution.py:33
  113.4 2.2 collective-permute-start
  115.6 1.3 collective-permute-start.1
  116.9 1.7 collective-permute-done.1
  118.7 3.4 %collective-permute-start.2 = (f32[130,1]{1,0:T(8,128)S(1)}, f32[130,1]{1,0:T(8,128)S(1)}, u32[]{:S(2)}, u32[]{:S(2)}) collective-permute-start(f32[130,1]{1,0:T(8,128)S(1)} %get-tuple-element.223), channel_id=1, source_target_pairs={{0,1},{1,2},{2,3},{4,5},{5,6},{6,7},{8,9},{9,10},{10,11},{12,13},{... | collective-permute-start | bytes 1568 | tf_op jit(solution)/shard_map/ppermute | solution.py:15
  122.1 1.3 collective-permute-start.3
  124.1 4.3 %collective-permute-done.3 = f32[130,1]{1,0:T(8,128)S(1)} collective-permute-done((f32[130,1]{1,0:T(8,128)S(1)}, f32[130,1]{1,0:T(8,128)S(1)}, u32[]{:S(2)}, u32[]{:S(2)}) %collective-permute-start.3) | collective-permute-done | bytes 552 | tf_op jit(solution)/shard_map/ppermute | solution.py:18
  128.5 23.2 %while.30 = (s32[]{:T(128)}, bf16[4,32,16,64]{3,2,0,1:T(8,128)(2,1)S(1)}, s32[4]{0:T(128)S(1)}, f32[1,130,130]{2,1,0:T(8,128)S(1)}, f32[32,9]{0,1:T(8,128)S(1)},...) while((s32[]{:T(128)}, ...), condition=%wide.region_4.5_spmd, body=%wide.region_2.4_spmd.sunk | while | flops 14647306 | bytes 2885173 | solution.py:74
  131.6 2.5 %reduce_max.42 = bf16[32,16,64]{0,2,1:T(8,128)(2,1)S(1)} reduce(bf16[32,16,2,64,2]{0,4,3,2,1:T(2,128)(2,1)S(1)} %bitcast.115, bf16[]{:T(256)} %constant.179..sunk), dimensions={2,4}, to_apply=%region_3.3 | reduce | flops 98304 | bytes 327682 | tf_op jit(solution)/shard_map/while/body/eval_jaxpr/reduce_max | solution.py:69
  137.4 2.5 %reduce_max.42 = bf16[32,16,64]{0,2,1:T(8,128)(2,1)S(1)} reduce(bf16[32,16,2,64,2]{0,4,3,2,1:T(2,128)(2,1)S(1)} %bitcast.115, bf16[]{:T(256)} %constant.179..sunk), dimensions={2,4}, to_apply=%region_3.3 | reduce | flops 98304 | bytes 327682 | tf_op jit(solution)/shard_map/while/body/eval_jaxpr/reduce_max | solution.py:69
  143.2 2.5 %reduce_max.42 = bf16[32,16,64]{0,2,1:T(8,128)(2,1)S(1)} reduce(bf16[32,16,2,64,2]{0,4,3,2,1:T(2,128)(2,1)S(1)} %bitcast.115, bf16[]{:T(256)} %constant.179..sunk), dimensions={2,4}, to_apply=%region_3.3 | reduce | flops 98304 | bytes 327682 | tf_op jit(solution)/shard_map/while/body/eval_jaxpr/reduce_max | solution.py:69
  149.0 2.5 %reduce_max.42 = bf16[32,16,64]{0,2,1:T(8,128)(2,1)S(1)} reduce(bf16[32,16,2,64,2]{0,4,3,2,1:T(2,128)(2,1)S(1)} %bitcast.115, bf16[]{:T(256)} %constant.179..sunk), dimensions={2,4}, to_apply=%region_3.3 | reduce | flops 98304 | bytes 327682 | tf_op jit(solution)/shard_map/while/body/eval_jaxpr/reduce_max | solution.py:69
  151.7 2.7 %collective-permute-start.4 = (bf16[32,1,64]{2,1,0:T(2,128)(2,1)S(1)}, bf16[32,1,64]{2,1,0:T(2,128)(2,1)S(1)}, u32[]{:S(2)}, u32[]{:S(2)}) collective-permute-start(bf16[32,1,64]{2,1,0:T(2,128)(2,1)S(1)} %get-tuple-element.217), channel_id=1, source_target_pairs={{0,4},{4,8},{8,12},{1,5},{5,9},{9,13},{2,6},{6,10},{10,14},{3,7},{... | collective-permute-start | bytes 12296 | tf_op jit(solution)/shard_map/ppermute | solution.py:15
  154.5 1.3 collective-permute-start.5
  155.8 2.7 %collective-permute-done.5 = bf16[32,1,64]{2,1,0:T(2,128)(2,1)S(1)} collective-permute-done((bf16[32,1,64]{2,1,0:T(2,128)(2,1)S(1)}, bf16[32,1,64]{2,1,0:T(2,128)(2,1)S(1)}, u32[]{:S(2)}, u32[]{:S(2)}) %collective-permute-start.5) | collective-permute-done | bytes 4128 | tf_op jit(solution)/shard_map/ppermute | solution.py:18
  159.3 3.4 %collective-permute-start.6 = (bf16[32,66,1]{1,0,2:T(8,128)(2,1)S(1)}, bf16[32,66,1]{1,0,2:T(8,128)(2,1)S(1)}, u32[]{:S(2)}, u32[]{:S(2)}) collective-permute-start(bf16[32,66,1]{1,0,2:T(8,128)(2,1)S(1)} %copy.64), channel_id=1, source_target_pairs={{0,1},{1,2},{2,3},{4,5},{5,6},{6,7},{8,9},{9,10},{10,11},{12,13},{... | collective-permute-start | bytes 12680 | tf_op jit(solution)/shard_map/ppermute | solution.py:15
  163.1 1.5 collective-permute-start.7
  164.8 0.9 copy.66
  165.7 2.9 %collective-permute-done.7 = bf16[32,66,1]{1,0,2:T(8,128)(2,1)S(1)} collective-permute-done((bf16[32,66,1]{1,0,2:T(8,128)(2,1)S(1)}, bf16[32,66,1]{1,0,2:T(8,128)(2,1)S(1)}, u32[]{:S(2)}, u32[]{:S(2)}) %collective-permute-start.7) | collective-permute-done | bytes 4256 | tf_op jit(solution)/shard_map/ppermute | solution.py:18
  168.6 0.9 copy.68
  170.1 32.3 %while.31 = (s32[]{:T(128)}, bf16[4,64,8,32]{1,3,2,0:T(8,128)(2,1)}, s32[4]{0:T(128)S(1)}, bf16[32,66,66]{2,0,1:T(8,128)(2,1)S(1)}, bf16[64,288]{1,0:T(8,128)(2,...) while((s32[]{:T(128)}, ...), condition=%wide.region_7.8_spmd, body=%wide.region_5.7_spmd.sunk | while | flops 37994504 | bytes 4822013 | solution.py:74
  173.1 0.8 copy.113
  174.0 2.4 concatenate.35
  181.2 0.8 copy.113
  182.1 2.4 concatenate.35
  189.3 0.8 copy.113
  190.1 2.4 concatenate.35
  197.4 0.8 copy.113
  198.2 2.4 concatenate.35
  201.8 0.6 bitcast_dynamic-update-slice_fusion.2
  202.4 0.7 fusion.14
  203.1 2.9 %collective-permute-start.8 = (bf16[64,1,32]{0,2,1:T(8,128)(2,1)S(1)}, bf16[64,1,32]{0,2,1:T(8,128)(2,1)S(1)}, u32[]{:S(2)}, u32[]{:S(2)}) collective-permute-start(bf16[64,1,32]{0,2,1:T(8,128)(2,1)S(1)} %get-tuple-element.221), channel_id=1, source_target_pairs={{0,4},{4,8},{8,12},{1,5},{5,9},{9,13},{2,6},{6,10},{10,14},{3,7},{... | collective-permute-start | bytes 12296 | tf_op jit(solution)/shard_map/ppermute | solution.py:15
  206.1 1.3 collective-permute-start.9
  208.1 2.0 collective-permute-done.9
  210.1 0.9 pad_maximum_fusion.6
  211.0 3.4 %collective-permute-start.10 = (bf16[64,34,1]{0,2,1:T(2,128)(2,1)S(1)}, bf16[64,34,1]{0,2,1:T(2,128)(2,1)S(1)}, u32[]{:S(2)}, u32[]{:S(2)}) collective-permute-start(bf16[64,34,1]{0,2,1:T(2,128)(2,1)S(1)} %get-tuple-element.219), channel_id=1, source_target_pairs={{0,1},{1,2},{2,3},{4,5},{5,6},{6,7},{8,9},{9,10},{10,11},{12,13},{... | collective-permute-start | bytes 13064 | tf_op jit(solution)/shard_map/ppermute | solution.py:15
  214.4 1.3 collective-permute-start.11
  215.8 1.1 copy.71
  217.5 2.6 %collective-permute-done.11 = bf16[64,34,1]{0,2,1:T(2,128)(2,1)S(1)} collective-permute-done((bf16[64,34,1]{0,2,1:T(2,128)(2,1)S(1)}, bf16[64,34,1]{0,2,1:T(2,128)(2,1)S(1)}, u32[]{:S(2)}, u32[]{:S(2)}) %collective-permute-start.11) | collective-permute-done | bytes 4384 | tf_op jit(solution)/shard_map/ppermute | solution.py:18
  220.1 1.1 pad_maximum_fusion.2
  221.2 4.8 %while.32 = (s32[]{:T(128)}, bf16[2,128,16,32]{1,3,2,0:T(8,128)(2,1)S(1)}, s32[2]{0:T(128)S(1)}, bf16[64,34,34]{0,2,1:T(8,128)(2,1)S(1)}, bf16[128,576]{1,0:T(8,...) while((s32[]{:T(128)}, ...), condition=%wide.region_9.10_spmd, body=%wide.region_8.9_spmd.sunk | while | flops 75694088 | bytes 3490551 | solution.py:74
  226.6 8.5 %pmax.7 = f32[32,2]{0,1:T(2,128)S(1)} all-reduce(f32[32,2]{0,1:T(2,128)S(1)} %select_reduce_fusion), channel_id=1, replica_groups=mesh['groups'=2,'qry'=4,'ref'=4] {'ref'}, use_global_device_ids=true, to_apply=%region_12.13 | all-reduce | flops 64 | bytes 512 | tf_op jit(solution)/shard_map/pmax | solution.py:144
  235.2 5.8 %psum.7 = f32[2]{0:T(128)S(1)} all-reduce(f32[2]{0:T(128)S(1)} %select_reduce_fusion.1), channel_id=1, replica_groups=mesh['groups'=2,'qry'=4,'ref'=4] {'qry'}, use_global_device_ids=true, to_apply=%region_14.15 | all-reduce | flops 2 | bytes 16 | tf_op jit(solution)/shard_map/psum | solution.py:147
  (183 shorter events, 33.6 us)
Async XLA Ops:
  7.2 218.9 %copy-start = (bf16[128]{0:T(256)(128)(2,1)S(1)}, bf16[128]{0:T(256)(128)(2,1)}, u32[]{:S(2)}) copy-start(bf16[128]{0:T(256)(128)(2,1)} %param.30) | copy-start | bytes 772
  7.2 66.0 %all-gather.2.cloned.1.call-start = ((), (), s32[]{:S(2)}) async-start(), calls=%async_computation | async-start | bytes 11059200 | tf_op jit(solution)/shard_map/all_gather | solution.py:109
  94.5 28.9 %copy-start.6 = (f32[3,3,32]{2,1,0:T(4,128)S(1)}, f32[3,3,32]{2,1,0:T(4,128)}, u32[]{:S(2)}) copy-start(f32[3,3,32]{2,1,0:T(4,128)} %param.24) | copy-start | bytes 3460
  94.5 29.0 %copy-start.7 = (s32[2]{0:T(128)S(1)}, s32[2]{0:T(128)}, u32[]{:S(2)}) copy-start(s32[2]{0:T(128)} %param.22) | copy-start | bytes 28
  94.5 34.0 %copy-start.5 = (f32[32]{0:T(128)S(1)}, f32[32]{0:T(128)}, u32[]{:S(2)}) copy-start(f32[32]{0:T(128)} %param.25) | copy-start | bytes 388
  113.4 3.5 %collective-permute-start = (f32[1,128]{1,0:T(1,128)S(1)}, f32[1,128]{1,0:T(1,128)S(1)}, u32[]{:S(2)}, u32[]{:S(2)}) collective-permute-start(f32[1,128]{1,0:T(1,128)S(1)} %get-tuple-element.225), channel_id=1, source_target_pairs={{0,4},{4,8},{8,12},{1,5},{5,9},{9,13},{2,6},{6,10},{10,14},{3,7},{... | collective-permute-start | bytes 1544 | tf_op jit(solution)/shard_map/ppermute | solution.py:15
  115.6 3.1 %collective-permute-start.1 = (f32[1,128]{1,0:T(1,128)S(1)}, f32[1,128]{1,0:T(1,128)S(1)}, u32[]{:S(2)}, u32[]{:S(2)}) collective-permute-start(f32[1,128]{1,0:T(1,128)S(1)} %get-tuple-element.226), channel_id=1, source_target_pairs={{4,0},{8,4},{12,8},{5,1},{9,5},{13,9},{6,2},{10,6},{14,10},{7,3},{... | collective-permute-start | bytes 1544 | tf_op jit(solution)/shard_map/ppermute | solution.py:18
  118.7 5.3 %collective-permute-start.2 = (f32[130,1]{1,0:T(8,128)S(1)}, f32[130,1]{1,0:T(8,128)S(1)}, u32[]{:S(2)}, u32[]{:S(2)}) collective-permute-start(f32[130,1]{1,0:T(8,128)S(1)} %get-tuple-element.223), channel_id=1, source_target_pairs={{0,1},{1,2},{2,3},{4,5},{5,6},{6,7},{8,9},{9,10},{10,11},{12,13},{... | collective-permute-start | bytes 1568 | tf_op jit(solution)/shard_map/ppermute | solution.py:15
  122.1 6.2 %collective-permute-start.3 = (f32[130,1]{1,0:T(8,128)S(1)}, f32[130,1]{1,0:T(8,128)S(1)}, u32[]{:S(2)}, u32[]{:S(2)}) collective-permute-start(f32[130,1]{1,0:T(8,128)S(1)} %get-tuple-element.224), channel_id=1, source_target_pairs={{1,0},{2,1},{3,2},{5,4},{6,5},{7,6},{9,8},{10,9},{11,10},{13,12},{... | collective-permute-start | bytes 1568 | tf_op jit(solution)/shard_map/ppermute | solution.py:18
  128.5 36.1 %copy-start.1 = (bf16[3,3,64,32]{2,3,1,0:T(8,128)(2,1)S(1)}, bf16[3,3,64,32]{2,3,1,0:T(8,128)(2,1)}, u32[]{:S(2)}) copy-start(bf16[3,3,64,32]{2,3,1,0:T(8,128)(2,1)} %param.26) | copy-start | bytes 110596
  151.7 18.4 %copy-start.3 = (f32[64]{0:T(128)S(1)}, f32[64]{0:T(128)}, u32[]{:S(2)}) copy-start(f32[64]{0:T(128)} %param.27) | copy-start | bytes 772
  151.7 4.1 %collective-permute-start.4 = (bf16[32,1,64]{2,1,0:T(2,128)(2,1)S(1)}, bf16[32,1,64]{2,1,0:T(2,128)(2,1)S(1)}, u32[]{:S(2)}, u32[]{:S(2)}) collective-permute-start(bf16[32,1,64]{2,1,0:T(2,128)(2,1)S(1)} %get-tuple-element.217), channel_id=1, source_target_pairs={{0,4},{4,8},{8,12},{1,5},{5,9},{9,13},{2,6},{6,10},{10,14},{3,7},{... | collective-permute-start | bytes 12296 | tf_op jit(solution)/shard_map/ppermute | solution.py:15
  154.5 4.1 %collective-permute-start.5 = (bf16[32,1,64]{2,1,0:T(2,128)(2,1)S(1)}, bf16[32,1,64]{2,1,0:T(2,128)(2,1)S(1)}, u32[]{:S(2)}, u32[]{:S(2)}) collective-permute-start(bf16[32,1,64]{2,1,0:T(2,128)(2,1)S(1)} %get-tuple-element.218), channel_id=1, source_target_pairs={{4,0},{8,4},{12,8},{5,1},{9,5},{13,9},{6,2},{10,6},{14,10},{7,3},{... | collective-permute-start | bytes 12296 | tf_op jit(solution)/shard_map/ppermute | solution.py:18
  159.3 5.4 %collective-permute-start.6 = (bf16[32,66,1]{1,0,2:T(8,128)(2,1)S(1)}, bf16[32,66,1]{1,0,2:T(8,128)(2,1)S(1)}, u32[]{:S(2)}, u32[]{:S(2)}) collective-permute-start(bf16[32,66,1]{1,0,2:T(8,128)(2,1)S(1)} %copy.64), channel_id=1, source_target_pairs={{0,1},{1,2},{2,3},{4,5},{5,6},{6,7},{8,9},{9,10},{10,11},{12,13},{... | collective-permute-start | bytes 12680 | tf_op jit(solution)/shard_map/ppermute | solution.py:15
  163.1 5.5 %collective-permute-start.7 = (bf16[32,66,1]{1,0,2:T(8,128)(2,1)S(1)}, bf16[32,66,1]{1,0,2:T(8,128)(2,1)S(1)}, u32[]{:S(2)}, u32[]{:S(2)}) collective-permute-start(bf16[32,66,1]{1,0,2:T(8,128)(2,1)S(1)} %copy.65), channel_id=1, source_target_pairs={{1,0},{2,1},{3,2},{5,4},{6,5},{7,6},{9,8},{10,9},{11,10},{13,12},{... | collective-permute-start | bytes 12680 | tf_op jit(solution)/shard_map/ppermute | solution.py:18
  170.1 51.1 %copy-start.4 = (f32[128]{0:T(128)S(1)}, f32[128]{0:T(128)}, u32[]{:S(2)}) copy-start(f32[128]{0:T(128)} %param.29) | copy-start | bytes 1540
  203.1 5.0 %collective-permute-start.8 = (bf16[64,1,32]{0,2,1:T(8,128)(2,1)S(1)}, bf16[64,1,32]{0,2,1:T(8,128)(2,1)S(1)}, u32[]{:S(2)}, u32[]{:S(2)}) collective-permute-start(bf16[64,1,32]{0,2,1:T(8,128)(2,1)S(1)} %get-tuple-element.221), channel_id=1, source_target_pairs={{0,4},{4,8},{8,12},{1,5},{5,9},{9,13},{2,6},{6,10},{10,14},{3,7},{... | collective-permute-start | bytes 12296 | tf_op jit(solution)/shard_map/ppermute | solution.py:15
  206.1 4.0 %collective-permute-start.9 = (bf16[64,1,32]{0,2,1:T(8,128)(2,1)S(1)}, bf16[64,1,32]{0,2,1:T(8,128)(2,1)S(1)}, u32[]{:S(2)}, u32[]{:S(2)}) collective-permute-start(bf16[64,1,32]{0,2,1:T(8,128)(2,1)S(1)} %get-tuple-element.222), channel_id=1, source_target_pairs={{4,0},{8,4},{12,8},{5,1},{9,5},{13,9},{6,2},{10,6},{14,10},{7,3},{... | collective-permute-start | bytes 12296 | tf_op jit(solution)/shard_map/ppermute | solution.py:18
  211.0 6.5 %collective-permute-start.10 = (bf16[64,34,1]{0,2,1:T(2,128)(2,1)S(1)}, bf16[64,34,1]{0,2,1:T(2,128)(2,1)S(1)}, u32[]{:S(2)}, u32[]{:S(2)}) collective-permute-start(bf16[64,34,1]{0,2,1:T(2,128)(2,1)S(1)} %get-tuple-element.219), channel_id=1, source_target_pairs={{0,1},{1,2},{2,3},{4,5},{5,6},{6,7},{8,9},{9,10},{10,11},{12,13},{... | collective-permute-start | bytes 13064 | tf_op jit(solution)/shard_map/ppermute | solution.py:15
  214.4 5.6 %collective-permute-start.11 = (bf16[64,34,1]{0,2,1:T(2,128)(2,1)S(1)}, bf16[64,34,1]{0,2,1:T(2,128)(2,1)S(1)}, u32[]{:S(2)}, u32[]{:S(2)}) collective-permute-start(bf16[64,34,1]{0,2,1:T(2,128)(2,1)S(1)} %get-tuple-element.220), channel_id=1, source_target_pairs={{1,0},{2,1},{3,2},{5,4},{6,5},{7,6},{9,8},{10,9},{11,10},{13,12},{... | collective-permute-start | bytes 13064 | tf_op jit(solution)/shard_map/ppermute | solution.py:18
  226.5 15.1 %copy-start.2 = (f32[32,32]{1,0:T(8,128)}, f32[32,32]{1,0:T(8,128)S(1)}, u32[]{:S(2)}) copy-start(f32[32,32]{1,0:T(8,128)S(1)} %broadcast_add_fusion) | copy-start | bytes 12292
Sparse Core Ops, SparseCore 0:
  9.5 63.5 all-gather.1
where the time goes:
time: 250 us; the launch traced here: 248 us
  waiting for transfers between devices  80 us (32%)
  local copies, waits for them, and re-layouts  63.7 us (25%)
  starting transfers between devices  26 us (10%)
  matrix products  23.9 us (10%)
  between operations  17.1 us (7%)
  other arithmetic  16.3 us (7%)
  blocking collectives  14.3 us (6%)
  loops' own time  7.15 us (3%)
    all_gather x1, waiting for transfers between devices, body(): shards = lax.all_gather(ref_feats, 'qry', axis=1, tiled=True)  62.7 us
    dot_general x1, matrix products, frame_sims(): lax.dot_general(query_mat, ref_mat, (((1,), (1,)), ((), ())), preferred_e...  18.8 us
    ppermute x6, starting transfers between devices, padded_2(): lax.ppermute(lax.slice_in_dim(block, block.shape[dim] - width, None, axis...  18 us
    ppermute x6, waiting for transfers between devices, padded_2(): lax.ppermute(lax.slice_in_dim(block, 0, width, axis=dim), axis, backward)  16.2 us
    dot_general x1, local copies, waits for them, and re-layouts, frame_sims(): lax.dot_general(query_mat, ref_mat, (((1,), (1,)), ((), ())), preferred_e...  12.7 us
    reduce_max x8, other arithmetic, one_block(): jnp.max(result.reshape(outputs, block_rows // 2, 2, width // 2, 2), axis=...  12.3 us
    while x76, local copies, waits for them, and re-layouts  11.5 us
    concatenate x10, local copies, waits for them, and re-layouts, one_block(): jnp.concatenate([window[:, shift_row:shift_row + block_rows, shift_col:sh...  11 us
  transfers between devices with their start and end apart: 13, of which 8 were waited for; matrix products, arithmetic and copies ran while one was open for 2% of the time, Pallas kernels for 0%

commit v1 on v0

--- a/solution.py
+++ b/solution.py
@@ -1,3 +1,4 @@
+import functools
 import math
 import jax
 import jax.numpy as jnp
@@ -5,6 +6,27 @@
 from jax.sharding import PartitionSpec as P
 
 MOST = 1
+
+
+def put_numbers(vec, which_dim):
+    chips = lax.psum(1, "qry")
+    y2 = range(1, chips)
+    long_array = map(lambda to_i: (to_i - 1, to_i), y2)
+    met_up = vec
+    found = [met_up]
+    tick = 0
+    kept_arr = list(long_array) + [(chips - 1, 0)]
+    while tick < chips - 1:
+        met_up = lax.ppermute(met_up, "qry", kept_arr)
+        found += [met_up]
+        tick = tick + 1
+    e_next = jnp.concatenate([*reversed(found)], axis=which_dim)
+    f_next = lax.axis_index("qry")
+    e_now = jnp.roll(e_next, shift=(f_next + 1) * met_up.shape[which_dim], axis=which_dim)
+    return e_now
+
+
+search_sources_all_for = functools.partial(put_numbers, which_dim=1)
 
 
 def padded_2(block, sides, width):
@@ -106,7 +128,7 @@
         0
     ]
     chosen, picked = slot_table(own_mask, MOST)
-    shards = lax.all_gather(ref_feats, "qry", axis=1, tiled=True)
+    shards = search_sources_all_for(ref_feats)
     senders = shards.shape[1]
     sims = frame_sims(query_mat, shards.reshape(tile_rows * senders * regions, channels), regions)
     sims = sims.reshape(1, frames, tile_rows, senders)

time: 250 us -> 394 us (1.58)
  local copies, waits for them, and re-layouts: 63.7 us -> 204 us
  other arithmetic: 16.3 us -> 40.6 us
  between operations: 17.1 us -> 3.69 us
  waiting for transfers between devices: 80 us -> 70.5 us
    reshape x0 -> x3, local copies, waits for them, and re-layouts: none -> 107 us  [the longest x1 76.5 us: frame_sims(): best = jnp.max(products.reshape(frames, regions, others, regions), axis=3)]
    all_gather x1 -> x0, waiting for transfers between devices: 62.7 us -> none  [body(): shards = lax.all_gather(ref_feats, 'qry', axis=1, tiled=True)]
    ppermute x0 -> x3, waiting for transfers between devices: none -> 53.8 us  [put_numbers(): met_up = lax.ppermute(met_up, 'qry', kept_arr)]
    unnamed x16 -> x30, local copies, waits for them, and re-layouts: 0.04 us -> 29 us
    reduce_max x0 -> x1, other arithmetic: none -> 24.1 us  [frame_sims(): best = jnp.max(products.reshape(frames, regions, others, regions), axis=3)]
    dynamic_slice x0 -> x2, local copies, waits for them, and re-layouts: none -> 17.6 us  [put_numbers(): jnp.roll(e_next, shift=(f_next + 1) * met_up.shape[which_dim], axis=which...]
    all_gather x1 -> x0, local copies, waits for them, and re-layouts: 8.6 us -> none  [body(): shards = lax.all_gather(ref_feats, 'qry', axis=1, tiled=True)]
    dot_general x1, local copies, waits for them, and re-layouts: 12.7 us -> 6.91 us  [frame_sims(): lax.dot_general(query_mat, ref_mat, (((1,), (1,)), ((), ())), preferred_e...]
  transfers between devices with their start and end apart: 13 -> 15, of which waited for: 8 -> 9; matrix products, arithmetic and copies ran while one was open for 2% -> 8% of each run, Pallas kernels for 0% -> 0%
where the time goes in v1:
time: 394 us; the launch traced here: 392 us
  local copies, waits for them, and re-layouts  204 us (52%)
  waiting for transfers between devices  70.5 us (18%)
  other arithmetic  40.6 us (10%)
  starting transfers between devices  28.6 us (7%)
  matrix products  22.7 us (6%)
  blocking collectives  14.3 us (4%)
  loops' own time  7.29 us (2%)
    reshape x1, local copies, waits for them, and re-layouts, frame_sims(): best = jnp.max(products.reshape(frames, regions, others, regions), axis=3)  76.5 us
    ppermute x3, waiting for transfers between devices, put_numbers(): met_up = lax.ppermute(met_up, 'qry', kept_arr)  53.8 us
    unnamed x30, local copies, waits for them, and re-layouts  29 us
    reduce_max x1, other arithmetic, frame_sims(): best = jnp.max(products.reshape(frames, regions, others, regions), axis=3)  24.1 us
    ppermute x6, starting transfers between devices, padded_2(): lax.ppermute(lax.slice_in_dim(block, block.shape[dim] - width, None, axis...  20.1 us
    dot_general x1, matrix products, frame_sims(): lax.dot_general(query_mat, ref_mat, (((1,), (1,)), ((), ())), preferred_e...  17.7 us
    dynamic_slice x2, local copies, waits for them, and re-layouts, put_numbers(): jnp.roll(e_next, shift=(f_next + 1) * met_up.shape[which_dim], axis=which...  17.6 us
    ppermute x6, waiting for transfers between devices, padded_2(): lax.ppermute(lax.slice_in_dim(block, 0, width, axis=dim), axis, backward)  16.4 us
  transfers between devices with their start and end apart: 15, of which 9 were waited for; matrix products, arithmetic and copies ran while one was open for 8% of the time, Pallas kernels for 0%

profile of v1, /device:TPU:0, one launch (start us, length us, event | category | flops | bytes accessed | tf_op | source)
XLA Modules:
  0.0 392.0 jit_solution(6632788764710456163)
XLA Ops:
  1.2 27.1 %collective-permute-done = bf16[32,1,9,3840]{3,0,2,1:T(8,128)(2,1)S(1)} collective-permute-done((bf16[32,1,9,3840]{3,0,2,1:T(8,128)(2,1)}, bf16[32,1,9,3840]{3,0,2,1:T(8,128)(2,1)S(1)}, u32[]{:S(2)}, u32[]{:S(2)}) %collective-permute-start) | collective-permute-done | bytes 2211872 | tf_op jit(solution)/shard_map/ppermute | solution.py:20
  28.3 1.3 copy-done.2
  29.6 26.8 %collective-permute-done.1 = bf16[32,1,9,3840]{3,0,2,1:T(8,128)(2,1)} collective-permute-done((bf16[32,1,9,3840]{3,0,2,1:T(8,128)(2,1)S(1)}, bf16[32,1,9,3840]{3,0,2,1:T(8,128)(2,1)}, u32[]{:S(2)}, u32[]{:S(2)}) %collective-permute-start.1) | collective-permute-done | bytes 2211872 | tf_op jit(solution)/shard_map/ppermute | solution.py:20
  56.4 10.2 %copy.70 = bf16[128,9,3840]{2,1,0:T(8,128)(2,1)} copy(bf16[128,9,3840]{2,0,1:T(8,128)(2,1)} %param.19) | data formatting | bytes 17694720 | tf_op args[0]
  66.6 15.1 %reshape.192 = bf16[1152,3840]{1,0:T(8,128)(2,1)} reshape(bf16[128,9,3840]{2,1,0:T(8,128)(2,1)} %copy.70) | data formatting | bytes 17694720 | tf_op jit(solution)/shard_map/reshape | solution.py:126
  81.7 1.4 dynamic_slice.28
  84.4 3.3 constant_dynamic-update-slice_fusion.18
  87.7 3.1 constant_dynamic-update-slice_fusion.17
  90.8 1.6 constant_dynamic-update-slice_fusion.16
  92.4 1.6 constant_dynamic-update-slice_fusion.15
  94.0 3.2 constant_dynamic-update-slice_fusion.14
  97.2 3.2 constant_dynamic-update-slice_fusion.13
  100.4 1.5 constant_dynamic-update-slice_fusion.12
  101.9 1.5 constant_dynamic-update-slice_fusion.11
  103.3 7.5 %constant_dynamic-slice_fusion.18 = bf16[32,4,9,3840]{3,0,2,1:T(8,128)(2,1)} fusion(bf16[32,8,9,3840]{3,0,2,1:T(8,128)(2,1)} %constant_dynamic-update-slice_fusion.11, s32[]{:T(128)S(6)} %select_n.37), kind=kLoop, calls=%fused_computation.65 | loop fusion | bytes 17694724 | tf_op jit(solution)/shard_map/jit(_roll_dynamic)/dynamic_slice | solution.py:25
  110.8 10.2 %copy.69 = bf16[32,4,9,3840]{3,2,1,0:T(8,128)(2,1)} copy(bf16[32,4,9,3840]{3,0,2,1:T(8,128)(2,1)} %constant_dynamic-slice_fusion.18) | data formatting | bytes 17694720 | tf_op jit(solution)/shard_map/jit(_roll_dynamic)/dynamic_slice | solution.py:25
  121.0 15.1 %reshape.191 = bf16[1152,3840]{1,0:T(8,128)(2,1)} reshape(bf16[32,4,9,3840]{3,2,1,0:T(8,128)(2,1)} %copy.69) | data formatting | bytes 17694720 | tf_op jit(solution)/shard_map/reshape | solution.py:133
  136.1 17.7 %convolution_bitcast_fusion = f32[1152,1152]{0,1:T(8,128)} fusion(bf16[1152,3840]{1,0:T(8,128)(2,1)} %reshape.191, bf16[1152,3840]{1,0:T(8,128)(2,1)} %reshape.192), kind=kOutput, calls=%fused_computation.38 | convolution fusion | flops 10192158720 | bytes 23003136 | tf_op jit(solution)/shard_map/dot_general | solution.py:55
  153.8 6.9 %copy.71 = f32[1152,1152]{1,0:T(8,128)} copy(f32[1152,1152]{0,1:T(8,128)} %convolution_bitcast_fusion) | data formatting | bytes 10616832 | tf_op jit(solution)/shard_map/dot_general | solution.py:55
  160.7 76.5 %reshape.193 = f32[128,9,128,9]{3,2,1,0:T(8,128)} reshape(f32[1152,1152]{1,0:T(8,128)} %copy.71) | data formatting | bytes 10616832 | tf_op jit(solution)/shard_map/reshape | solution.py:60
  237.2 24.1 %reduce_max.36 = f32[128,9,128]{2,1,0:T(8,128)S(1)} reduce(f32[128,9,128,9]{3,2,1,0:T(8,128)} %reshape.193, f32[]{:T(128)} %constant.107.clone.1), dimensions={3}, to_apply=%region_0.0 | reduce | flops 1179648 | bytes 5898244 | tf_op jit(solution)/shard_map/reduce_max | solution.py:60
  261.6 4.3 %collective-permute-start.3 = (f32[1,128]{1,0:T(1,128)S(1)}, f32[1,128]{1,0:T(1,128)S(1)}, u32[]{:S(2)}, u32[]{:S(2)}) collective-permute-start(f32[1,128]{1,0:T(1,128)S(1)} %get-tuple-element.225), channel_id=1, source_target_pairs={{0,4},{4,8},{8,12},{1,5},{5,9},{9,13},{2,6},{6,10},{10,14},{3,7},{... | collective-permute-start | bytes 1544 | tf_op jit(solution)/shard_map/ppermute | solution.py:37
  267.2 1.7 collective-permute-done.4
  269.1 3.5 collective-permute-start.5
  272.5 1.5 collective-permute-start.6
  274.5 4.4 %collective-permute-done.6 = f32[130,1]{1,0:T(8,128)S(1)} collective-permute-done((f32[130,1]{1,0:T(8,128)S(1)}, f32[130,1]{1,0:T(8,128)S(1)}, u32[]{:S(2)}, u32[]{:S(2)}) %collective-permute-start.6) | collective-permute-done | bytes 552 | tf_op jit(solution)/shard_map/ppermute | solution.py:40
  279.0 23.2 %while.30 = (s32[]{:T(128)}, bf16[4,32,16,64]{3,2,0,1:T(8,128)(2,1)S(1)}, s32[4]{0:T(128)S(1)}, f32[1,130,130]{2,1,0:T(8,128)S(1)}, f32[32,9]{0,1:T(8,128)S(1)},...) while((s32[]{:T(128)}, ...), condition=%wide.region_4.5_spmd, body=%wide.region_2.4_spmd.sunk | while | flops 14647306 | bytes 2885173 | solution.py:96
  282.1 2.5 reduce_max.41
  287.9 2.5 reduce_max.41
  293.7 2.5 reduce_max.41
  299.5 2.5 reduce_max.41
  302.2 2.4 collective-permute-start.7
  304.6 1.3 collective-permute-start.8
  305.9 2.6 collective-permute-done.8
  309.4 3.5 collective-permute-start.9
  315.7 3.0 collective-permute-done.10
  320.2 32.4 %while.31 = (s32[]{:T(128)}, bf16[4,64,8,32]{1,3,2,0:T(8,128)(2,1)}, s32[4]{0:T(128)S(1)}, bf16[32,66,66]{2,0,1:T(8,128)(2,1)S(1)}, bf16[64,288]{1,0:T(8,128)(2,...) while((s32[]{:T(128)}, ...), condition=%wide.region_7.8_spmd, body=%wide.region_5.7_spmd.sunk | while | flops 37994504 | bytes 4822013 | solution.py:96
  324.1 2.4 concatenate.42
  332.2 2.4 concatenate.42
  340.3 2.4 concatenate.42
  348.4 2.4 concatenate.42
  353.3 2.9 collective-permute-start.11
  358.3 2.0 collective-permute-done.12
  361.2 3.5 collective-permute-start.13
  367.8 2.6 collective-permute-done.14
  371.5 5.0 %while.32 = (s32[]{:T(128)}, bf16[2,128,16,32]{1,3,2,0:T(8,128)(2,1)S(1)}, s32[2]{0:T(128)S(1)}, bf16[64,34,34]{0,2,1:T(8,128)(2,1)S(1)}, bf16[128,576]{1,0:T(8,...) while((s32[]{:T(128)}, ...), condition=%wide.region_9.10_spmd, body=%wide.region_8.9_spmd.sunk | while | flops 75694088 | bytes 3490551 | solution.py:96
  377.1 8.5 %pmax.7 = f32[32,2]{0,1:T(2,128)S(1)} all-reduce(f32[32,2]{0,1:T(2,128)S(1)} %select_reduce_fusion), channel_id=1, replica_groups=mesh['groups'=2,'qry'=4,'ref'=4] {'ref'}, use_global_device_ids=true, to_apply=%region_12.13 | all-reduce | flops 64 | bytes 512 | tf_op jit(solution)/shard_map/pmax | solution.py:166
  385.7 5.8 %psum.7 = f32[2]{0:T(128)S(1)} all-reduce(f32[2]{0:T(128)S(1)} %select_reduce_fusion.1), channel_id=1, replica_groups=mesh['groups'=2,'qry'=4,'ref'=4] {'qry'}, use_global_device_ids=true, to_apply=%region_14.15 | all-reduce | flops 2 | bytes 16 | tf_op jit(solution)/shard_map/psum | solution.py:169
  (206 shorter events, 49.1 us)
Async XLA Ops:
  0.6 375.9 %copy-start = (bf16[128]{0:T(256)(128)(2,1)S(1)}, bf16[128]{0:T(256)(128)(2,1)}, u32[]{:S(2)}) copy-start(bf16[128]{0:T(256)(128)(2,1)} %param.30) | copy-start | bytes 772
  0.6 27.6 %collective-permute-start = (bf16[32,1,9,3840]{3,0,2,1:T(8,128)(2,1)}, bf16[32,1,9,3840]{3,0,2,1:T(8,128)(2,1)S(1)}, u32[]{:S(2)}, u32[]{:S(2)}) collective-permute-start(bf16[32,1,9,3840]{3,0,2,1:T(8,128)(2,1)} %param.20), channel_id=1, source_target_pairs={{0,4},{4,8},{8,12},{12,0},{1,5},{5,9},{9,13},{13,1},{2,6},{6,10},{... | collective-permute-start | bytes 6635528 | tf_op jit(solution)/shard_map/ppermute | solution.py:20
  28.3 1.3 copy-start.2
  29.6 26.8 %collective-permute-start.1 = (bf16[32,1,9,3840]{3,0,2,1:T(8,128)(2,1)S(1)}, bf16[32,1,9,3840]{3,0,2,1:T(8,128)(2,1)}, u32[]{:S(2)}, u32[]{:S(2)}) collective-permute-start(bf16[32,1,9,3840]{3,0,2,1:T(8,128)(2,1)S(1)} %collective-permute-done), channel_id=1, source_target_pairs={{0,4},{4,8},{8,12},{12,0},{1,5},{5,9},{9,13},{13,1},{2,6},{6,10},{... | collective-permute-start | bytes 6635528 | tf_op jit(solution)/shard_map/ppermute | solution.py:20
  56.4 28.0 %collective-permute-start.2 = (bf16[32,1,9,3840]{3,0,2,1:T(8,128)(2,1)}, bf16[32,1,9,3840]{3,0,2,1:T(8,128)(2,1)}, u32[]{:S(2)}, u32[]{:S(2)}) collective-permute-start(bf16[32,1,9,3840]{3,0,2,1:T(8,128)(2,1)} %collective-permute-done.1), channel_id=1, source_target_pairs={{0,4},{4,8},{8,12},{12,0},{1,5},{5,9},{9,13},{13,1},{2,6},{6,10},{... | collective-permute-start | bytes 6635528 | tf_op jit(solution)/shard_map/ppermute | solution.py:20
  81.7 10.7 %copy-start.1 = (bf16[32,1,9,3840]{3,0,2,1:T(8,128)(2,1)S(1)}, bf16[32,1,9,3840]{3,0,2,1:T(8,128)(2,1)}, u32[]{:S(2)}) copy-start(bf16[32,1,9,3840]{3,0,2,1:T(8,128)(2,1)} %param.20) | copy-start | bytes 6635524
  84.4 6.4 %copy-start.3 = (bf16[32,1,9,3840]{3,0,2,1:T(8,128)(2,1)S(1)}, bf16[32,1,9,3840]{3,0,2,1:T(8,128)(2,1)}, u32[]{:S(2)}) copy-start(bf16[32,1,9,3840]{3,0,2,1:T(8,128)(2,1)} %copy-done.2) | copy-start | bytes 6635524
  237.2 36.8 %copy-start.9 = (f32[3,3,32]{2,1,0:T(4,128)S(1)}, f32[3,3,32]{2,1,0:T(4,128)}, u32[]{:S(2)}) copy-start(f32[3,3,32]{2,1,0:T(4,128)} %param.24) | copy-start | bytes 3460
  237.2 36.8 %copy-start.10 = (s32[2]{0:T(128)S(1)}, s32[2]{0:T(128)}, u32[]{:S(2)}) copy-start(s32[2]{0:T(128)} %param.22) | copy-start | bytes 28
  237.2 41.8 %copy-start.8 = (f32[32]{0:T(128)S(1)}, f32[32]{0:T(128)}, u32[]{:S(2)}) copy-start(f32[32]{0:T(128)} %param.25) | copy-start | bytes 388
  261.6 5.6 %collective-permute-start.3 = (f32[1,128]{1,0:T(1,128)S(1)}, f32[1,128]{1,0:T(1,128)S(1)}, u32[]{:S(2)}, u32[]{:S(2)}) collective-permute-start(f32[1,128]{1,0:T(1,128)S(1)} %get-tuple-element.225), channel_id=1, source_target_pairs={{0,4},{4,8},{8,12},{1,5},{5,9},{9,13},{2,6},{6,10},{10,14},{3,7},{... | collective-permute-start | bytes 1544 | tf_op jit(solution)/shard_map/ppermute | solution.py:37
  265.9 3.1 collective-permute-start.4
  269.1 5.4 %collective-permute-start.5 = (f32[130,1]{1,0:T(8,128)S(1)}, f32[130,1]{1,0:T(8,128)S(1)}, u32[]{:S(2)}, u32[]{:S(2)}) collective-permute-start(f32[130,1]{1,0:T(8,128)S(1)} %get-tuple-element.223), channel_id=1, source_target_pairs={{0,1},{1,2},{2,3},{4,5},{5,6},{6,7},{8,9},{9,10},{10,11},{12,13},{... | collective-permute-start | bytes 1568 | tf_op jit(solution)/shard_map/ppermute | solution.py:37
  272.5 6.3 %collective-permute-start.6 = (f32[130,1]{1,0:T(8,128)S(1)}, f32[130,1]{1,0:T(8,128)S(1)}, u32[]{:S(2)}, u32[]{:S(2)}) collective-permute-start(f32[130,1]{1,0:T(8,128)S(1)} %get-tuple-element.224), channel_id=1, source_target_pairs={{1,0},{2,1},{3,2},{5,4},{6,5},{7,6},{9,8},{10,9},{11,10},{13,12},{... | collective-permute-start | bytes 1568 | tf_op jit(solution)/shard_map/ppermute | solution.py:40
  279.0 35.5 %copy-start.4 = (bf16[3,3,64,32]{2,3,1,0:T(8,128)(2,1)S(1)}, bf16[3,3,64,32]{2,3,1,0:T(8,128)(2,1)}, u32[]{:S(2)}) copy-start(bf16[3,3,64,32]{2,3,1,0:T(8,128)(2,1)} %param.26) | copy-start | bytes 110596
  302.2 18.0 %copy-start.6 = (f32[64]{0:T(128)S(1)}, f32[64]{0:T(128)}, u32[]{:S(2)}) copy-start(f32[64]{0:T(128)} %param.27) | copy-start | bytes 772
  302.2 3.7 collective-permute-start.7
  304.6 4.0 %collective-permute-start.8 = (bf16[32,1,64]{2,1,0:T(2,128)(2,1)S(1)}, bf16[32,1,64]{2,1,0:T(2,128)(2,1)S(1)}, u32[]{:S(2)}, u32[]{:S(2)}) collective-permute-start(bf16[32,1,64]{2,1,0:T(2,128)(2,1)S(1)} %get-tuple-element.218), channel_id=1, source_target_pairs={{4,0},{8,4},{12,8},{5,1},{9,5},{13,9},{6,2},{10,6},{14,10},{7,3},{... | collective-permute-start | bytes 12296 | tf_op jit(solution)/shard_map/ppermute | solution.py:40
  309.4 5.3 %collective-permute-start.9 = (bf16[32,66,1]{1,0,2:T(8,128)(2,1)S(1)}, bf16[32,66,1]{1,0,2:T(8,128)(2,1)S(1)}, u32[]{:S(2)}, u32[]{:S(2)}) collective-permute-start(bf16[32,66,1]{1,0,2:T(8,128)(2,1)S(1)} %copy.74), channel_id=1, source_target_pairs={{0,1},{1,2},{2,3},{4,5},{5,6},{6,7},{8,9},{9,10},{10,11},{12,13},{... | collective-permute-start | bytes 12680 | tf_op jit(solution)/shard_map/ppermute | solution.py:37
  313.2 5.5 %collective-permute-start.10 = (bf16[32,66,1]{1,0,2:T(8,128)(2,1)S(1)}, bf16[32,66,1]{1,0,2:T(8,128)(2,1)S(1)}, u32[]{:S(2)}, u32[]{:S(2)}) collective-permute-start(bf16[32,66,1]{1,0,2:T(8,128)(2,1)S(1)} %copy.75), channel_id=1, source_target_pairs={{1,0},{2,1},{3,2},{5,4},{6,5},{7,6},{9,8},{10,9},{11,10},{13,12},{... | collective-permute-start | bytes 12680 | tf_op jit(solution)/shard_map/ppermute | solution.py:40
  320.2 51.2 %copy-start.7 = (f32[128]{0:T(128)S(1)}, f32[128]{0:T(128)}, u32[]{:S(2)}) copy-start(f32[128]{0:T(128)} %param.29) | copy-start | bytes 1540
  353.3 5.0 %collective-permute-start.11 = (bf16[64,1,32]{0,2,1:T(8,128)(2,1)S(1)}, bf16[64,1,32]{0,2,1:T(8,128)(2,1)S(1)}, u32[]{:S(2)}, u32[]{:S(2)}) collective-permute-start(bf16[64,1,32]{0,2,1:T(8,128)(2,1)S(1)} %get-tuple-element.221), channel_id=1, source_target_pairs={{0,4},{4,8},{8,12},{1,5},{5,9},{9,13},{2,6},{6,10},{10,14},{3,7},{... | collective-permute-start | bytes 12296 | tf_op jit(solution)/shard_map/ppermute | solution.py:37
  356.3 4.0 %collective-permute-start.12 = (bf16[64,1,32]{0,2,1:T(8,128)(2,1)S(1)}, bf16[64,1,32]{0,2,1:T(8,128)(2,1)S(1)}, u32[]{:S(2)}, u32[]{:S(2)}) collective-permute-start(bf16[64,1,32]{0,2,1:T(8,128)(2,1)S(1)} %get-tuple-element.222), channel_id=1, source_target_pairs={{4,0},{8,4},{12,8},{5,1},{9,5},{13,9},{6,2},{10,6},{14,10},{7,3},{... | collective-permute-start | bytes 12296 | tf_op jit(solution)/shard_map/ppermute | solution.py:40
  361.2 6.6 %collective-permute-start.13 = (bf16[64,34,1]{0,2,1:T(2,128)(2,1)S(1)}, bf16[64,34,1]{0,2,1:T(2,128)(2,1)S(1)}, u32[]{:S(2)}, u32[]{:S(2)}) collective-permute-start(bf16[64,34,1]{0,2,1:T(2,128)(2,1)S(1)} %get-tuple-element.219), channel_id=1, source_target_pairs={{0,1},{1,2},{2,3},{4,5},{5,6},{6,7},{8,9},{9,10},{10,11},{12,13},{... | collective-permute-start | bytes 13064 | tf_op jit(solution)/shard_map/ppermute | solution.py:37
  364.7 5.6 %collective-permute-start.14 = (bf16[64,34,1]{0,2,1:T(2,128)(2,1)S(1)}, bf16[64,34,1]{0,2,1:T(2,128)(2,1)S(1)}, u32[]{:S(2)}, u32[]{:S(2)}) collective-permute-start(bf16[64,34,1]{0,2,1:T(2,128)(2,1)S(1)} %get-tuple-element.220), channel_id=1, source_target_pairs={{1,0},{2,1},{3,2},{5,4},{6,5},{7,6},{9,8},{10,9},{11,10},{13,12},{... | collective-permute-start | bytes 13064 | tf_op jit(solution)/shard_map/ppermute | solution.py:40
  377.0 15.1 %copy-start.5 = (f32[32,32]{1,0:T(8,128)}, f32[32,32]{1,0:T(8,128)S(1)}, u32[]{:S(2)}) copy-start(f32[32,32]{1,0:T(8,128)S(1)} %broadcast_add_fusion) | copy-start | bytes 12292
